TPU v7x, 32 devices: a whole 2x2x4 slice. The times are simulated.
32 devices in a mesh: wide: 4 (over y, x), grp: 8 (over z, core).
Axes of the slice: x: 2, y: 2, z: 4, core: 2. Of those that a mesh axis runs over, the one named last changes fastest.
Arguments:
- shapes: float32 [64, 3, 312], P(('wide', 'grp')), may hold values from -10 to 10
- density: float32 [64, 3, 312], P(('wide', 'grp')), may hold values from -6 to 6
- quad_weight: float32 [64, 312], P(('wide', 'grp')), may hold values from 0.013 to 0.13
- live: int32 [64], P(('wide', 'grp')), may hold values from 0 to 1, as said below
- neighbor: int32 [64, 64], P(('wide', 'grp')), may hold values from 0 to 1
- rotation: bfloat16 [312, 312], replicated, may hold values from 0 to 1
Outputs:
- self_ops: bfloat16 [64, 3, 312, 3, 312], P(('wide', 'grp'))
- velocity: float32 [64, 3, 312], P(('wide', 'grp'))
Inputs may be any that keep to these rules, and one draw needn't show every extreme that they name: Exactly 8 of the 16 slots held by the devices of one index of wide are live.
All inputs are finite; a program needn't handle non-finite values.
Results may differ from a plain program's by a relative error of at most 0.0036.
Values may be sent and summed in bfloat16 or wider, within the bound.
A program may use at most 64 MiB of HBM per device.

v0:
```python
import jax
import jax.numpy as jnp
from jax import lax
from jax.sharding import PartitionSpec as P

soft_square = 0.0625


def kernel_block(targets, quad_nodes, weights):
    offset = targets[:, :, :, None] - quad_nodes[:, :, None, :]
    dist_sq = jnp.sum(offset * offset, axis=1)
    inv_cube = lax.rsqrt(dist_sq + soft_square) ** 3
    scaled = inv_cube * weights[:, None, :]
    outer_prod = offset[:, :, None] * offset[:, None, :]
    unit_eye = jnp.eye(3, dtype=jnp.float32)
    kernel_full = (
        unit_eye[None, :, :, None, None] * (dist_sq + 2.0 * soft_square)[:, None, None] + outer_prod
    ) * scaled[:, None, None]
    return kernel_full.transpose(0, 1, 3, 2, 4)


def build_ops(targets, shapes, weights, rotation):
    rot_wide = rotation.astype(jnp.float32)
    quad_nodes = jnp.einsum("cak,jk->caj", shapes, rot_wide, precision=lax.Precision.HIGHEST)
    kernel = kernel_block(targets, quad_nodes, weights).astype(jnp.bfloat16)
    leading = kernel.shape[:4]
    flattened = kernel.reshape(-1, kernel.shape[4])
    product = jnp.dot(flattened, rotation, preferred_element_type=jnp.float32)
    return product.reshape(leading + (rotation.shape[1],)).astype(jnp.bfloat16)


def pair_velocity(targets, src_position, src_strength):
    offset = targets[:, :, None] - src_position[:, None, :]
    dist_sq = jnp.sum(offset * offset, axis=0)
    inv_cube = lax.rsqrt(dist_sq + soft_square) ** 3
    projected = jnp.sum(offset * src_strength[:, None, :], axis=0)
    pair_terms = (
        src_strength[:, None, :] * (dist_sq + 2.0 * soft_square)[None] + offset * projected[None]
    ) * inv_cube[None]
    return jnp.sum(pair_terms, axis=2)


def live_order(row_live):
    group_rows = row_live.shape[0]
    live_count = group_rows // 2
    live_int = row_live.astype(jnp.int32)
    live_rank = jnp.cumsum(live_int) - 1
    pick_rows = jnp.arange(live_count, dtype=jnp.int32)
    chosen = (pick_rows[:, None] == live_rank[None, :]) & (live_int[None, :] > 0)
    slot_ids = jnp.sum(
        jnp.where(chosen, jnp.arange(group_rows, dtype=jnp.int32)[None, :], 0), axis=1
    )
    return (live_int, jnp.clip(live_rank, 0, live_count - 1), slot_ids)


def on_device(shapes, density, quad_weight, live, neighbor, rotation):
    slot_count = shapes.shape[0]
    points = shapes.shape[2]
    grp_count = lax.axis_size("grp")
    grp_pos = lax.axis_index("grp")
    wide_pos = lax.axis_index("wide")
    live_f = live.astype(jnp.float32)
    mask_f = neighbor.astype(jnp.float32)
    strength = quad_weight[:, None, :] * density * live_f[:, None, None]
    row_shapes, row_live, row_mask = (
        lax.all_gather(shapes, "grp", axis=0, tiled=True),
        lax.all_gather(live_f, "grp", axis=0, tiled=True),
        lax.all_gather(mask_f, "grp", axis=0, tiled=True),
    )
    live_int, rank_safe, slot_ids = live_order(row_live)
    picked_shapes = jnp.take(row_shapes, slot_ids, axis=0)

    def one_slot(element):
        shape_one, weight_one, live_flag = element
        return lax.cond(
            live_flag > 0,
            lambda: build_ops(shape_one[None], shape_one[None], weight_one[None], rotation)[0],
            lambda: jnp.zeros((3, points, 3, points), jnp.bfloat16),
        )

    self_ops = lax.map(one_slot, (shapes, quad_weight, live))
    dens_half = density.astype(jnp.bfloat16)
    self_velocity = jnp.einsum(
        "kaibj,kbj->kai", self_ops, dens_half, preferred_element_type=jnp.float32
    )
    src_position, src_strength = (
        lax.all_gather(shapes, "wide", axis=0, tiled=True),
        lax.all_gather(strength, "wide", axis=0, tiled=True),
    )
    group_rows = row_shapes.shape[0]
    live_count = slot_ids.shape[0]
    source_count = src_position.shape[0]
    source_ids = jnp.arange(source_count, dtype=jnp.int32)
    columns = (
        source_ids // slot_count * grp_count + grp_pos
    ) * slot_count + source_ids % slot_count
    live_mask = jnp.take(row_mask, slot_ids, axis=0)
    pair_mask = jnp.take(live_mask, columns, axis=1)
    target_ids = wide_pos * group_rows + slot_ids
    pair_mask = jnp.where(
        target_ids[:, None] == columns[None, :], jnp.zeros_like(pair_mask), pair_mask
    )
    flat_targets = picked_shapes.transpose(1, 0, 2).reshape(3, live_count * points)

    def add_source(source, running):
        velocity_part = pair_velocity(
            flat_targets, src_position[source], src_strength[source]
        ).reshape(3, live_count, points)
        return running + velocity_part * pair_mask[:, source][None, :, None]

    compact_part = lax.fori_loop(
        0, source_count, add_source, jnp.zeros((3, live_count, points), jnp.float32)
    )
    partial_value = jnp.take(compact_part, rank_safe, axis=1)
    partial_value = jnp.where(
        live_int[None, :, None] > 0, partial_value, jnp.zeros_like(partial_value)
    )
    mutual = lax.psum_scatter(partial_value, "grp", scatter_dimension=1, tiled=True)
    velocity = (self_velocity + mutual.transpose(1, 0, 2)) * live_f[:, None, None]
    return (self_ops, velocity)


def solution(mesh):
    placed = (
        P(("wide", "grp"), None, None),
        P(("wide", "grp"), None, None),
        P(("wide", "grp"), None),
        P(("wide", "grp")),
        P(("wide", "grp"), None),
        P(),
    )
    return jax.shard_map(
        on_device,
        mesh=mesh,
        in_specs=placed,
        out_specs=(P(("wide", "grp"), None, None, None, None), P(("wide", "grp"), None, None)),
        check_vma=False,
    )
```

profile of v0, /device:TPU:0, one launch (start us, length us, event | category | flops | bytes accessed | tf_op | source)
XLA Modules:
  0.0 159.4 jit_solution(5382423423938834347)
XLA Ops:
  0.6 1.4 fusion.36
  3.5 18.1 %all-reduce = f32[16]{0:T(128)S(1)} all-reduce(f32[16]{0:T(128)S(1)} %convert_dynamic-update-slice_fusion), channel_id=1, replica_groups=mesh['wide'=4,'grp'=8] {'grp'}, use_global_device_ids=true, to_apply=%add | all-reduce | flops 16 | bytes 128
  22.6 8.4 %all-gather = f32[8,2,64]{2,1,0:T(2,128)S(1)} all-gather(f32[1,2,64]{2,1,0:T(2,128)S(1)} %convert_bitcast_fusion.2), channel_id=1, replica_groups=mesh['wide'=4,'grp'=8] {'grp'}, dimensions={0}, use_global_device_ids=true | all-gather | bytes 4608 | tf_op jit(solution)/shard_map/all_gather | solution.py:68
  33.2 13.9 %all_gather.17 = f32[16,3,312]{2,1,0:T(4,128)S(1)} all-gather(f32[2,3,312]{2,1,0:T(4,128)S(1)} %copy.31), channel_id=1, replica_groups=mesh['wide'=4,'grp'=8] {'grp'}, dimensions={0}, use_global_device_ids=true | all-gather | bytes 67392 | tf_op jit(solution)/shard_map/all_gather | solution.py:66
  47.8 8.2 %all_gather.18 = f32[8,3,312]{2,1,0:T(4,128)S(1)} all-gather(f32[2,3,312]{2,1,0:T(4,128)S(1)} %copy.31), channel_id=1, replica_groups=mesh['wide'=4,'grp'=8] {'wide'}, dimensions={0}, use_global_device_ids=true | all-gather | bytes 37440 | tf_op jit(solution)/shard_map/all_gather | solution.py:87
  57.4 8.2 %all_gather.16 = f32[8,3,312]{2,1,0:T(4,128)S(1)} all-gather(f32[2,3,312]{2,1,0:T(4,128)S(1)} %fusion.21), channel_id=1, replica_groups=mesh['wide'=4,'grp'=8] {'wide'}, dimensions={0}, use_global_device_ids=true | all-gather | bytes 37440 | tf_op jit(solution)/shard_map/all_gather | solution.py:88
  65.7 49.6 %while.25 = (s32[]{:T(128)}, f32[3,8,312]{2,1,0:T(8,128)S(1)}, f32[8,3,312]{2,1,0:T(4,128)S(1)}, f32[3,8,312]{2,1,0:T(8,128)S(1)}, f32[8,3,312]{2,1,0:T(4,128)S(...) while((s32[]{:T(128)}, f32[3,8,312]{2,1,0:T(8,128)S(1)}, f32[8,3,312]{2,1,0:T(4,128)S(1)}, ...), condition=%wide.region_11.12_spmd.clone, body=%wide.region_7.11_spmd.clone.sunk | while | flops 27271296 | bytes 25249732 | solution.py:111
  65.8 1.7 %fusion.44 = (f32[2496,312]{0,1:T(8,128)S(1)}, f32[2496,312]{0,1:T(8,128)S(1)}) fusion(f32[3,312]{1,0:T(4,128)S(1)} %get-tuple-element.381, f32[3,2496]{1,0:T(4,128)S(1)} %sub.165, f32[3,312]{1,0:T(4,128)S(1)} %get-tuple-element.382), kind=kLoop, calls=%fused_computation.8.clone.1 | loop fusion | flops 10123776 | bytes 6267456 | tf_op jit(solution)/shard_map/while/body/eval_jaxpr/reduce_sum | solution.py:36
  68.3 3.3 %fusion.45 = f32[3,2496]{1,0:T(4,128)S(1)} fusion(f32[2496,312]{0,1:T(8,128)S(1)} %get-tuple-element.384, f32[2496,312]{0,1:T(8,128)S(1)} %get-tuple-element.385, f32[2496,312]{0,1:T(8,128)S(1)} %get-tuple-element.386, f32[3,312]{1,0:T(4,128)S(1)} %get-tuple-element.381, f32[3,2496]{1,0:T(4,128)S(1)} %sub.165, f32[3,312]{1,0:T(4,128)S(1)} %get-tuple-element.382), kind=kLoop, calls=%fused_computation.11.clone.1 | loop fusion | flops 14010048 | bytes 9412416 | tf_op jit(solution)/shard_map/while/body/eval_jaxpr/reduce_sum | solution.py:40
  72.0 1.7 %fusion.44 = (f32[2496,312]{0,1:T(8,128)S(1)}, f32[2496,312]{0,1:T(8,128)S(1)}) fusion(f32[3,312]{1,0:T(4,128)S(1)} %get-tuple-element.381, f32[3,2496]{1,0:T(4,128)S(1)} %sub.165, f32[3,312]{1,0:T(4,128)S(1)} %get-tuple-element.382), kind=kLoop, calls=%fused_computation.8.clone.1 | loop fusion | flops 10123776 | bytes 6267456 | tf_op jit(solution)/shard_map/while/body/eval_jaxpr/reduce_sum | solution.py:36
  74.5 3.3 %fusion.45 = f32[3,2496]{1,0:T(4,128)S(1)} fusion(f32[2496,312]{0,1:T(8,128)S(1)} %get-tuple-element.384, f32[2496,312]{0,1:T(8,128)S(1)} %get-tuple-element.385, f32[2496,312]{0,1:T(8,128)S(1)} %get-tuple-element.386, f32[3,312]{1,0:T(4,128)S(1)} %get-tuple-element.381, f32[3,2496]{1,0:T(4,128)S(1)} %sub.165, f32[3,312]{1,0:T(4,128)S(1)} %get-tuple-element.382), kind=kLoop, calls=%fused_computation.11.clone.1 | loop fusion | flops 14010048 | bytes 9412416 | tf_op jit(solution)/shard_map/while/body/eval_jaxpr/reduce_sum | solution.py:40
  78.2 1.7 %fusion.44 = (f32[2496,312]{0,1:T(8,128)S(1)}, f32[2496,312]{0,1:T(8,128)S(1)}) fusion(f32[3,312]{1,0:T(4,128)S(1)} %get-tuple-element.381, f32[3,2496]{1,0:T(4,128)S(1)} %sub.165, f32[3,312]{1,0:T(4,128)S(1)} %get-tuple-element.382), kind=kLoop, calls=%fused_computation.8.clone.1 | loop fusion | flops 10123776 | bytes 6267456 | tf_op jit(solution)/shard_map/while/body/eval_jaxpr/reduce_sum | solution.py:36
  80.7 3.3 %fusion.45 = f32[3,2496]{1,0:T(4,128)S(1)} fusion(f32[2496,312]{0,1:T(8,128)S(1)} %get-tuple-element.384, f32[2496,312]{0,1:T(8,128)S(1)} %get-tuple-element.385, f32[2496,312]{0,1:T(8,128)S(1)} %get-tuple-element.386, f32[3,312]{1,0:T(4,128)S(1)} %get-tuple-element.381, f32[3,2496]{1,0:T(4,128)S(1)} %sub.165, f32[3,312]{1,0:T(4,128)S(1)} %get-tuple-element.382), kind=kLoop, calls=%fused_computation.11.clone.1 | loop fusion | flops 14010048 | bytes 9412416 | tf_op jit(solution)/shard_map/while/body/eval_jaxpr/reduce_sum | solution.py:40
  84.4 1.7 %fusion.44 = (f32[2496,312]{0,1:T(8,128)S(1)}, f32[2496,312]{0,1:T(8,128)S(1)}) fusion(f32[3,312]{1,0:T(4,128)S(1)} %get-tuple-element.381, f32[3,2496]{1,0:T(4,128)S(1)} %sub.165, f32[3,312]{1,0:T(4,128)S(1)} %get-tuple-element.382), kind=kLoop, calls=%fused_computation.8.clone.1 | loop fusion | flops 10123776 | bytes 6267456 | tf_op jit(solution)/shard_map/while/body/eval_jaxpr/reduce_sum | solution.py:36
  86.9 3.3 %fusion.45 = f32[3,2496]{1,0:T(4,128)S(1)} fusion(f32[2496,312]{0,1:T(8,128)S(1)} %get-tuple-element.384, f32[2496,312]{0,1:T(8,128)S(1)} %get-tuple-element.385, f32[2496,312]{0,1:T(8,128)S(1)} %get-tuple-element.386, f32[3,312]{1,0:T(4,128)S(1)} %get-tuple-element.381, f32[3,2496]{1,0:T(4,128)S(1)} %sub.165, f32[3,312]{1,0:T(4,128)S(1)} %get-tuple-element.382), kind=kLoop, calls=%fused_computation.11.clone.1 | loop fusion | flops 14010048 | bytes 9412416 | tf_op jit(solution)/shard_map/while/body/eval_jaxpr/reduce_sum | solution.py:40
  90.6 1.7 %fusion.44 = (f32[2496,312]{0,1:T(8,128)S(1)}, f32[2496,312]{0,1:T(8,128)S(1)}) fusion(f32[3,312]{1,0:T(4,128)S(1)} %get-tuple-element.381, f32[3,2496]{1,0:T(4,128)S(1)} %sub.165, f32[3,312]{1,0:T(4,128)S(1)} %get-tuple-element.382), kind=kLoop, calls=%fused_computation.8.clone.1 | loop fusion | flops 10123776 | bytes 6267456 | tf_op jit(solution)/shard_map/while/body/eval_jaxpr/reduce_sum | solution.py:36
  93.1 3.3 %fusion.45 = f32[3,2496]{1,0:T(4,128)S(1)} fusion(f32[2496,312]{0,1:T(8,128)S(1)} %get-tuple-element.384, f32[2496,312]{0,1:T(8,128)S(1)} %get-tuple-element.385, f32[2496,312]{0,1:T(8,128)S(1)} %get-tuple-element.386, f32[3,312]{1,0:T(4,128)S(1)} %get-tuple-element.381, f32[3,2496]{1,0:T(4,128)S(1)} %sub.165, f32[3,312]{1,0:T(4,128)S(1)} %get-tuple-element.382), kind=kLoop, calls=%fused_computation.11.clone.1 | loop fusion | flops 14010048 | bytes 9412416 | tf_op jit(solution)/shard_map/while/body/eval_jaxpr/reduce_sum | solution.py:40
  96.8 1.7 %fusion.44 = (f32[2496,312]{0,1:T(8,128)S(1)}, f32[2496,312]{0,1:T(8,128)S(1)}) fusion(f32[3,312]{1,0:T(4,128)S(1)} %get-tuple-element.381, f32[3,2496]{1,0:T(4,128)S(1)} %sub.165, f32[3,312]{1,0:T(4,128)S(1)} %get-tuple-element.382), kind=kLoop, calls=%fused_computation.8.clone.1 | loop fusion | flops 10123776 | bytes 6267456 | tf_op jit(solution)/shard_map/while/body/eval_jaxpr/reduce_sum | solution.py:36
  99.3 3.3 %fusion.45 = f32[3,2496]{1,0:T(4,128)S(1)} fusion(f32[2496,312]{0,1:T(8,128)S(1)} %get-tuple-element.384, f32[2496,312]{0,1:T(8,128)S(1)} %get-tuple-element.385, f32[2496,312]{0,1:T(8,128)S(1)} %get-tuple-element.386, f32[3,312]{1,0:T(4,128)S(1)} %get-tuple-element.381, f32[3,2496]{1,0:T(4,128)S(1)} %sub.165, f32[3,312]{1,0:T(4,128)S(1)} %get-tuple-element.382), kind=kLoop, calls=%fused_computation.11.clone.1 | loop fusion | flops 14010048 | bytes 9412416 | tf_op jit(solution)/shard_map/while/body/eval_jaxpr/reduce_sum | solution.py:40
  103.0 1.7 %fusion.44 = (f32[2496,312]{0,1:T(8,128)S(1)}, f32[2496,312]{0,1:T(8,128)S(1)}) fusion(f32[3,312]{1,0:T(4,128)S(1)} %get-tuple-element.381, f32[3,2496]{1,0:T(4,128)S(1)} %sub.165, f32[3,312]{1,0:T(4,128)S(1)} %get-tuple-element.382), kind=kLoop, calls=%fused_computation.8.clone.1 | loop fusion | flops 10123776 | bytes 6267456 | tf_op jit(solution)/shard_map/while/body/eval_jaxpr/reduce_sum | solution.py:36
  105.5 3.3 %fusion.45 = f32[3,2496]{1,0:T(4,128)S(1)} fusion(f32[2496,312]{0,1:T(8,128)S(1)} %get-tuple-element.384, f32[2496,312]{0,1:T(8,128)S(1)} %get-tuple-element.385, f32[2496,312]{0,1:T(8,128)S(1)} %get-tuple-element.386, f32[3,312]{1,0:T(4,128)S(1)} %get-tuple-element.381, f32[3,2496]{1,0:T(4,128)S(1)} %sub.165, f32[3,312]{1,0:T(4,128)S(1)} %get-tuple-element.382), kind=kLoop, calls=%fused_computation.11.clone.1 | loop fusion | flops 14010048 | bytes 9412416 | tf_op jit(solution)/shard_map/while/body/eval_jaxpr/reduce_sum | solution.py:40
  109.2 1.7 %fusion.44 = (f32[2496,312]{0,1:T(8,128)S(1)}, f32[2496,312]{0,1:T(8,128)S(1)}) fusion(f32[3,312]{1,0:T(4,128)S(1)} %get-tuple-element.381, f32[3,2496]{1,0:T(4,128)S(1)} %sub.165, f32[3,312]{1,0:T(4,128)S(1)} %get-tuple-element.382), kind=kLoop, calls=%fused_computation.8.clone.1 | loop fusion | flops 10123776 | bytes 6267456 | tf_op jit(solution)/shard_map/while/body/eval_jaxpr/reduce_sum | solution.py:36
  111.7 3.3 %fusion.45 = f32[3,2496]{1,0:T(4,128)S(1)} fusion(f32[2496,312]{0,1:T(8,128)S(1)} %get-tuple-element.384, f32[2496,312]{0,1:T(8,128)S(1)} %get-tuple-element.385, f32[2496,312]{0,1:T(8,128)S(1)} %get-tuple-element.386, f32[3,312]{1,0:T(4,128)S(1)} %get-tuple-element.381, f32[3,2496]{1,0:T(4,128)S(1)} %sub.165, f32[3,312]{1,0:T(4,128)S(1)} %get-tuple-element.382), kind=kLoop, calls=%fused_computation.11.clone.1 | loop fusion | flops 14010048 | bytes 9412416 | tf_op jit(solution)/shard_map/while/body/eval_jaxpr/reduce_sum | solution.py:40
  116.0 26.7 %all-reduce.1 = f32[3,16,312]{2,0,1:T(4,128)S(1)} all-reduce(f32[3,16,312]{2,0,1:T(4,128)S(1)} %select_bitcast_fusion), channel_id=2, replica_groups=mesh['wide'=4,'grp'=8] {'grp'}, use_global_device_ids=true, to_apply=%region_12.13.clone | all-reduce | flops 14976 | bytes 119808
  142.8 11.7 %while.24 = (s32[]{:T(128)}, bf16[2,3,312,3,312]{4,2,3,1,0:T(8,128)(2,1)}, s32[2]{0:T(128)S(1)}, f32[2,3,312]{2,1,0:T(4,128)S(1)}, bf16[312,312]{1,0:T(8,128)(2,...) while((s32[]{:T(128)}, bf16[2,3,312,3,312]{4,2,3,1,0:T(8,128)(2,1)}, s32[2]{0:T(128)S(1)}, ...), condition=%wide.region_4.5_spmd, body=%wide.region_0.4_spmd.sunk | while | flops 557002368 | bytes 10757255 | solution.py:81
  144.0 3.1 %conditional.2 = (bf16[1,3,312,3,312]{4,2,3,1,0:T(8,128)(2,1)S(1)}) conditional(s32[]{:T(128)} %bitcast.58, () %tuple.83, (f32[2,3,312]{2,1,0:T(4,128)S(1)}, s32[]{:T(128)}, bf16[312,312]{1,0:T(8,128)(2,1)S(1)}, f32[2,312]{1,0:T(2,128)S(1)}) %tuple.84), branch_computations={%region_1.1_spmd, %region_2.3_spmd} | conditional | flops 557002368 | bytes 6847864 | solution.py:75
  144.9 2.2 %convert_bitcast_fusion = bf16[1,3,312,3,312]{4,2,3,1,0:T(8,128)(2,1)S(1)} fusion(f32[312,312]{1,0:T(8,128)S(1)} %get-tuple-element.296, f32[3,312,312]{2,1,0:T(8,128)S(1)} %broadcast_subtract_fusion, f32[312,312]{1,0:T(8,128)S(1)} %get-tuple-element.295, f32[3,3]{1,0:T(4,128)S(1)} %fusion.18, bf16[312,312]{1,0:T(8,128)(2,1)S(1)} %get-tuple-element.166), kind=kOutput, calls=%fused_computation.22 | convolution fusion | flops 551940480 | bytes 3893796 | tf_op jit(solution)/shard_map/while/body/eval_jaxpr/cond/branch_1_fun/dot_general | solution.py:28
  147.1 1.6 constant_dynamic-update-slice_fusion.2
  149.8 3.1 %conditional.2 = (bf16[1,3,312,3,312]{4,2,3,1,0:T(8,128)(2,1)S(1)}) conditional(s32[]{:T(128)} %bitcast.58, () %tuple.83, (f32[2,3,312]{2,1,0:T(4,128)S(1)}, s32[]{:T(128)}, bf16[312,312]{1,0:T(8,128)(2,1)S(1)}, f32[2,312]{1,0:T(2,128)S(1)}) %tuple.84), branch_computations={%region_1.1_spmd, %region_2.3_spmd} | conditional | flops 557002368 | bytes 6847864 | solution.py:75
  150.7 2.2 %convert_bitcast_fusion = bf16[1,3,312,3,312]{4,2,3,1,0:T(8,128)(2,1)S(1)} fusion(f32[312,312]{1,0:T(8,128)S(1)} %get-tuple-element.296, f32[3,312,312]{2,1,0:T(8,128)S(1)} %broadcast_subtract_fusion, f32[312,312]{1,0:T(8,128)S(1)} %get-tuple-element.295, f32[3,3]{1,0:T(4,128)S(1)} %fusion.18, bf16[312,312]{1,0:T(8,128)(2,1)S(1)} %get-tuple-element.166), kind=kOutput, calls=%fused_computation.22 | convolution fusion | flops 551940480 | bytes 3893796 | tf_op jit(solution)/shard_map/while/body/eval_jaxpr/cond/branch_1_fun/dot_general | solution.py:28
  152.9 1.6 constant_dynamic-update-slice_fusion.2
  154.5 3.5 %fusion.22 = f32[2,1,3,312,1]{3,1,4,2,0:T(1,128)S(1)} fusion(bf16[2,3,312,3,312]{4,2,3,1,0:T(8,128)(2,1)} %get-tuple-element.261, bf16[2,3,312,1,1]{2,0,1,3,4:T(2,128)(2,1)S(1)} %convert_bitcast_fusion.1), kind=kOutput, calls=%fused_computation.47 | convolution fusion | flops 3504384 | bytes 3515616 | tf_op jit(solution)/shard_map/kaibj,kbj->kai/dot_general | solution.py:83
  (109 shorter events, 19.2 us)
Async XLA Ops:
  65.6 77.1 %copy-start = (bf16[312,312]{1,0:T(8,128)(2,1)S(1)}, bf16[312,312]{1,0:T(8,128)(2,1)}, u32[]{:S(2)}) copy-start(bf16[312,312]{1,0:T(8,128)(2,1)} %param.17) | copy-start | bytes 584068
  65.6 77.1 %copy-start.1 = (f32[2,312]{1,0:T(2,128)S(1)}, f32[2,312]{1,0:T(2,128)}, u32[]{:S(2)}) copy-start(f32[2,312]{1,0:T(2,128)} %param.14) | copy-start | bytes 7492
  65.6 77.1 %copy-start.3 = (s32[2]{0:T(128)S(1)}, s32[2]{0:T(128)}, u32[]{:S(2)}) copy-start(s32[2]{0:T(128)} %param.15) | copy-start | bytes 28
  142.8 11.7 %copy-start.2 = (f32[2,3,312]{2,0,1:T(2,128)S(1)}, f32[2,3,312]{2,0,1:T(2,128)}, u32[]{:S(2)}) copy-start(f32[2,3,312]{2,0,1:T(2,128)} %param.13) | copy-start | bytes 22468
where the time goes:
time: 157 us; the launch traced here: 159 us
  blocking collectives  83.6 us (53%)
  other arithmetic  52.4 us (33%)
  local copies, waits for them, and re-layouts  11.2 us (7%)
  matrix products  8.44 us (5%)
  between operations  2.17 us (1%)
  loops' own time  1.67 us (1%)
    unnamed x2, blocking collectives  44.8 us
    reduce_sum x8, other arithmetic, pair_velocity(): return jnp.sum(pair_terms, axis=2)  26.7 us
    all_gather x1, blocking collectives, on_device(): lax.all_gather(shapes, 'grp', axis=0, tiled=True)  13.9 us
    reduce_sum x8, other arithmetic, pair_velocity(): projected = jnp.sum(offset * src_strength[:, None, :], axis=0)  13.7 us
    all_gather x1, blocking collectives, on_device(): lax.all_gather(mask_f, 'grp', axis=0, tiled=True)  8.42 us
    all_gather x1, blocking collectives, on_device(): lax.all_gather(shapes, 'wide', axis=0, tiled=True)  8.24 us
    all_gather x1, blocking collectives, on_device(): lax.all_gather(strength, 'wide', axis=0, tiled=True)  8.2 us
    add x8, other arithmetic, pair_velocity(): dist_sq + 2.0 * soft_square  6.63 us

commit v1 on v0

v1 whole, which is shorter than its diff:
```python
import functools
import jax
import jax.numpy as jnp
from jax import lax
from jax.experimental import pallas as pl
from jax.experimental.pallas import tpu as pltpu
from jax.sharding import PartitionSpec as P

soft_square = 0.0625
MESH = pl.DeviceIdType.MESH
SYM = ((0, 0), (0, 1), (0, 2), (1, 1), (1, 2), (2, 2))


def up(value, step):
    return (value + step - 1) // step * step


def split3(x):
    hi = x.astype(jnp.bfloat16)
    rest = x - hi.astype(jnp.float32)
    mid = rest.astype(jnp.bfloat16)
    low = (rest - mid.astype(jnp.float32)).astype(jnp.bfloat16)
    return hi, mid, low


def gather_kernel(
    slots, grp, wide, rows,
    pk_ref, qw_ref, dens_ref, rot_ref,
    ops_ref, vel_ref, tgt_ref, src_ref, mask_ref,
    gbuf, wbuf, kern, cols, gsend, grecv, wsend, wrecv,
):
    n = rot_ref.shape[0]
    me_g = lax.axis_index("grp")
    me_w = lax.axis_index("wide")
    barrier = pltpu.get_barrier_semaphore()
    for off in range(1, grp):
        pl.semaphore_signal(
            barrier, inc=1, device_id={"grp": lax.rem(me_g + off, grp)}, device_id_type=MESH
        )
    for off in range(1, wide):
        pl.semaphore_signal(
            barrier, inc=1, device_id={"wide": lax.rem(me_w + off, wide)}, device_id_type=MESH
        )
    pl.semaphore_wait(barrier, grp + wide - 2)
    copies = []
    for off in range(1, grp):
        copies.append(
            pltpu.make_async_remote_copy(
                src_ref=pk_ref.at[pl.ds(0, rows)],
                dst_ref=gbuf.at[me_g],
                send_sem=gsend.at[off],
                recv_sem=grecv.at[off],
                device_id={"grp": lax.rem(me_g + off, grp)},
                device_id_type=MESH,
            )
        )
    for off in range(1, wide):
        copies.append(
            pltpu.make_async_remote_copy(
                src_ref=pk_ref,
                dst_ref=wbuf.at[me_w],
                send_sem=wsend.at[off],
                recv_sem=wrecv.at[off],
                device_id={"wide": lax.rem(me_w + off, wide)},
                device_id_type=MESH,
            )
        )
    for copy in copies:
        copy.start()

    rot = rot_ref[...]
    for c in range(slots):
        place = jnp.concatenate([pk_ref[a * slots + c : a * slots + c + 1, :] for a in range(3)], axis=0)
        pos = place[:, :n]
        nodes = None
        for piece in split3(pos):
            part = lax.dot_general(
                piece, rot, (((1,), (1,)), ((), ())), preferred_element_type=jnp.float32
            )
            nodes = part if nodes is None else nodes + part
        weight = qw_ref[c : c + 1, :]
        tall = jnp.concatenate([place, jnp.zeros((5, place.shape[1]), jnp.float32)], axis=0)
        cols[...] = jnp.transpose(tall)

        def chunk(step, carry):
            start = pl.multiple_of(step * 16, 16)
            block = cols[pl.ds(start, 16), :]
            diff = [block[:, a : a + 1] - nodes[a : a + 1, :] for a in range(3)]
            dist = diff[0] * diff[0] + diff[1] * diff[1] + diff[2] * diff[2]
            inv = lax.rsqrt(dist + soft_square)
            scaled = inv * inv * inv * weight
            half = [d * scaled for d in diff]
            diag = (dist + 2.0 * soft_square) * scaled
            for index, (a, b) in enumerate(SYM):
                value = half[a] * diff[b]
                if a == b:
                    value = value + diag
                kern[index, pl.ds(start, 16), :] = value.astype(jnp.bfloat16)
            return carry

        lax.fori_loop(0, kern.shape[1] // 16, chunk, 0)
        alive = pk_ref[rows + 3 * slots + c : rows + 3 * slots + c + 1, :n]
        dens = jnp.concatenate(
            [dens_ref[b * slots + c : b * slots + c + 1, :] for b in range(3)], axis=0
        )
        dens = jnp.concatenate([dens, jnp.zeros((5, n), jnp.float32)], axis=0).astype(jnp.bfloat16)
        total = [None] * 3
        for index, (a, b) in enumerate(SYM):
            product = jnp.dot(kern[index], rot, preferred_element_type=jnp.float32)
            made = jnp.where(alive > 0.0, product, 0.0).astype(jnp.bfloat16)[:n]
            ops_ref[c, index] = made
            part = lax.dot_general(
                dens, made, (((1,), (1,)), ((), ())), preferred_element_type=jnp.float32
            )
            pieces = [(a, part[b : b + 1])]
            if a != b:
                pieces.append((b, part[a : a + 1]))
            for k, piece in pieces:
                total[k] = piece if total[k] is None else total[k] + piece
        for a in range(3):
            vel_ref[a * slots + c : a * slots + c + 1, :] = total[a]

    gbuf[me_g] = pk_ref[0:rows]
    wbuf[me_w] = pk_ref[...]
    for copy in copies:
        copy.wait()
    tgt_ref[...] = gbuf[...]
    src_ref[...] = wbuf[...]
    width = mask_ref.shape[1]
    for g in range(grp):
        for c in range(slots):
            mask_ref[g * slots + c : g * slots + c + 1, :] = gbuf[
                g, 3 * slots + c : 3 * slots + c + 1, 0:width
            ].astype(jnp.int32)
    for w in range(wide):
        for c in range(slots):
            row = grp * slots + w * slots + c
            mask_ref[row : row + 1, :] = wbuf[
                w, rows + 3 * slots + c : rows + 3 * slots + c + 1, 0:width
            ].astype(jnp.int32)


def pair_kernel(
    slots, grp, wide, rows,
    mask_ref, ops_ref, tgt_ref, src_ref,
    out_ref, acc_ref, spread, flip, aim, heap, order, sems,
):
    n = ops_ref.shape[2]
    lanes = tgt_ref.shape[2]
    me_g = lax.axis_index("grp")
    me_w = lax.axis_index("wide")
    copies = []
    for c in range(slots):
        for a in range(3):
            for b in range(3):
                index = SYM.index((min(a, b), max(a, b)))
                copies.append(
                    pltpu.make_async_copy(
                        ops_ref.at[c, index], out_ref.at[c, a, b], sems.at[len(copies)]
                    )
                )
    for copy in copies:
        copy.start()
    acc_ref[...] = jnp.zeros_like(acc_ref)
    heap[...] = jnp.zeros_like(heap)
    group = grp * slots
    for t in range(group):
        for a in range(3):
            row = a * slots + t % slots
            aim[t, a] = jnp.broadcast_to(tgt_ref[t // slots, row : row + 1, :], (8, lanes))
    panel = wide * slots

    for w in range(wide):
        flip[...] = jnp.transpose(src_ref[w])
        for c in range(slots):

            @pl.when(mask_ref[group + w * slots + c, 0] > 0)
            def _():
                for k in range(6):
                    row = k * slots + c if k < 3 else rows + (k - 3) * slots + c
                    spread[w * slots + c, k] = jnp.broadcast_to(
                        flip[0:n, row : row + 1], (n, 128)
                    )

    def scan_target(t, count):
        for s in range(panel):
            column = (s // slots * grp + me_g) * slots + s % slots
            hit = (
                (mask_ref[t, column] > 0)
                & (mask_ref[group + s, 0] > 0)
                & (me_w * group + t != column)
            )
            order[count] = t * panel + s
            count = count + hit.astype(jnp.int32)
        return count

    count = lax.fori_loop(0, group, scan_target, jnp.int32(0))
    tiles = lanes // 128

    def one_pair(p, carry):
        code = order[p]
        t, s = code // panel, code % panel
        xs = [
            [aim[t, a, :, l * 128 : l * 128 + 128] for a in range(3)] for l in range(tiles)
        ]

        def step(j, sums):
            start = pl.multiple_of(j * 8, 8)
            y = [spread[s, a, pl.ds(start, 8), :] for a in range(3)]
            f = [spread[s, 3 + a, pl.ds(start, 8), :] for a in range(3)]
            fresh = []
            for l in range(tiles):
                d = [xs[l][a] - y[a] for a in range(3)]
                dist = (d[0] * d[0] + d[1] * d[1]) + d[2] * d[2] + soft_square
                inv = lax.rsqrt(dist)
                cube = inv * inv * inv
                dot = d[0] * f[0] + d[1] * f[1] + d[2] * f[2]
                near = (dist + soft_square) * cube
                far = dot * cube
                for a in range(3):
                    fresh.append(sums[l * 3 + a] + (f[a] * near + d[a] * far))
            return tuple(fresh)

        zero = tuple(jnp.zeros((8, 128), jnp.float32) for _ in range(3 * tiles))
        steps = n // 8
        sums = lax.fori_loop(0, steps, step, zero, unroll=3 if steps % 3 == 0 else 1)
        for l in range(tiles):
            for a in range(3):
                here = (t, a, slice(0, 8), slice(l * 128, l * 128 + 128))
                heap[here] = heap[here] + sums[l * 3 + a]
        return carry

    lax.fori_loop(0, count, one_pair, 0)
    for t in range(group):
        for a in range(3):
            row = a * slots + t % slots
            acc_ref[t // slots, row : row + 1, :] = jnp.sum(heap[t, a], axis=0, keepdims=True)
    for copy in copies:
        copy.wait()


def scatter_kernel(slots, grp, part_ref, self_ref, live_ref, vel_ref, got, send, recv):
    n = self_ref.shape[1]
    me = lax.axis_index("grp")
    barrier = pltpu.get_barrier_semaphore()
    for off in range(1, grp):
        pl.semaphore_signal(
            barrier, inc=1, device_id={"grp": lax.rem(me + off, grp)}, device_id_type=MESH
        )
    pl.semaphore_wait(barrier, grp - 1)
    copies = []
    for off in range(1, grp):
        peer = lax.rem(me + off, grp)
        copies.append(
            pltpu.make_async_remote_copy(
                src_ref=part_ref.at[peer],
                dst_ref=got.at[off],
                send_sem=send.at[off],
                recv_sem=recv.at[off],
                device_id={"grp": peer},
                device_id_type=MESH,
            )
        )
    for copy in copies:
        copy.start()
    total = part_ref[me]
    for index, copy in enumerate(copies):
        copy.wait()
        total = total + got[index + 1]
    vel = self_ref[...] + total[0 : 3 * slots, :n]
    for a in range(3):
        for c in range(slots):
            row = a * slots + c
            alive = live_ref[3 * slots + c : 3 * slots + c + 1, :n]
            vel_ref[row : row + 1, :] = vel[row : row + 1] * alive


def on_device(shapes, density, quad_weight, live, neighbor, rotation):
    slots, _, n = shapes.shape
    caps = neighbor.shape[1]
    grp = lax.axis_size("grp")
    wide = lax.axis_size("wide")
    rows = up(4 * slots, 8)
    lanes = up(max(n, caps), 128)
    width = up(caps, 128)
    tall = up(n, 16)
    live_f = live.astype(jnp.float32)
    strength = quad_weight[:, None, :] * density * live_f[:, None, None]

    def rows_of(value):
        value = value.transpose(1, 0, 2).reshape(3 * slots, n)
        return jnp.pad(value, ((0, 0), (0, lanes - n)))

    fill = jnp.zeros((rows - 4 * slots, lanes), jnp.float32)
    mask = jnp.pad(neighbor.astype(jnp.float32) * live_f[:, None], ((0, 0), (0, lanes - caps)))
    packed = jnp.concatenate(
        [
            rows_of(shapes), mask, fill,
            rows_of(strength), jnp.broadcast_to(live_f[:, None], (slots, lanes)), fill,
        ],
        axis=0,
    )
    flat_density = density.transpose(1, 0, 2).reshape(3 * slots, n)
    vmem = pl.BlockSpec(memory_space=pltpu.VMEM)
    any_space = pl.BlockSpec(memory_space=pl.ANY)
    ops6, self_velocity, targets, sources, flags = pl.pallas_call(
        functools.partial(gather_kernel, slots, grp, wide, rows),
        out_shape=(
            jax.ShapeDtypeStruct((slots, 6, n, n), jnp.bfloat16),
            jax.ShapeDtypeStruct((3 * slots, n), jnp.float32),
            jax.ShapeDtypeStruct((grp, rows, lanes), jnp.float32),
            jax.ShapeDtypeStruct((wide, 2 * rows, lanes), jnp.float32),
            jax.ShapeDtypeStruct(((grp + wide) * slots, width), jnp.int32),
        ),
        in_specs=[vmem] * 4,
        out_specs=(vmem,) * 5,
        scratch_shapes=[
            pltpu.VMEM((grp, rows, lanes), jnp.float32),
            pltpu.VMEM((wide, 2 * rows, lanes), jnp.float32),
            pltpu.VMEM((6, tall, n), jnp.bfloat16),
            pltpu.VMEM((lanes, 8), jnp.float32),
            pltpu.SemaphoreType.DMA((grp,)),
            pltpu.SemaphoreType.DMA((grp,)),
            pltpu.SemaphoreType.DMA((wide,)),
            pltpu.SemaphoreType.DMA((wide,)),
        ],
        compiler_params=pltpu.CompilerParams(collective_id=0, has_side_effects=True),
        name="gather_ops",
    )(packed, quad_weight, flat_density, rotation)
    blocks, partial = pl.pallas_call(
        functools.partial(pair_kernel, slots, grp, wide, rows),
        out_shape=(
            jax.ShapeDtypeStruct((slots, 3, 3, n, n), jnp.bfloat16),
            jax.ShapeDtypeStruct((grp, rows, lanes), jnp.float32),
        ),
        in_specs=[pl.BlockSpec(memory_space=pltpu.SMEM), vmem, vmem, vmem],
        out_specs=(any_space, vmem),
        scratch_shapes=[
            pltpu.VMEM((wide * slots, 6, n, 128), jnp.float32),
            pltpu.VMEM((lanes, 2 * rows), jnp.float32),
            pltpu.VMEM((grp * slots, 3, 8, lanes), jnp.float32),
            pltpu.VMEM((grp * slots, 3, 8, lanes), jnp.float32),
            pltpu.SMEM((grp * slots * wide * slots + 1,), jnp.int32),
            pltpu.SemaphoreType.DMA((9 * slots,)),
        ],
        name="pair_sums",
    )(flags, ops6, targets, sources)
    velocity = pl.pallas_call(
        functools.partial(scatter_kernel, slots, grp),
        out_shape=jax.ShapeDtypeStruct((3 * slots, n), jnp.float32),
        in_specs=[vmem] * 3,
        out_specs=vmem,
        scratch_shapes=[
            pltpu.VMEM((grp, rows, lanes), jnp.float32),
            pltpu.SemaphoreType.DMA((grp,)),
            pltpu.SemaphoreType.DMA((grp,)),
        ],
        compiler_params=pltpu.CompilerParams(collective_id=1, has_side_effects=True),
        name="scatter_sums",
    )(partial, self_velocity, packed[rows:])
    return (
        blocks.transpose(0, 1, 3, 2, 4),
        velocity.reshape(3, slots, n).transpose(1, 0, 2),
    )


def solution(mesh):
    placed = (
        P(("wide", "grp"), None, None),
        P(("wide", "grp"), None, None),
        P(("wide", "grp"), None),
        P(("wide", "grp")),
        P(("wide", "grp"), None),
        P(),
    )
    return jax.shard_map(
        on_device,
        mesh=mesh,
        in_specs=placed,
        out_specs=(P(("wide", "grp"), None, None, None, None), P(("wide", "grp"), None, None)),
        check_vma=False,
    )
```

time: 157 us -> 51 us (0.32); the launches traced: 159 us -> 51.8 us
  blocking collectives: 83.6 us -> 0 us
  other arithmetic: 52.4 us -> 3.4 us
  Pallas kernels: 0 us -> 44.4 us
  matrix products: 8.44 us -> 0 us
  local copies, waits for them, and re-layouts: 11.2 us -> 3.42 us
  loops' own time: 1.67 us -> 0 us
    unnamed x2 -> x0, blocking collectives: 44.8 us -> none
    pallas_call x0 -> x3, Pallas kernels: none -> 44.4 us  [the longest x1 19.1 us: on_device(): pl.pallas_call(functools.partial(scatter_kernel, slots, grp), out_shape=j...]
    reduce_sum x19 -> x0, other arithmetic: 41 us -> none  [the longest x8 26.7 us: pair_velocity(): return jnp.sum(pair_terms, axis=2)]
    all_gather x4 -> x0, blocking collectives: 38.8 us -> none  [the longest x1 13.9 us: on_device(): lax.all_gather(shapes, 'grp', axis=0, tiled=True)]
    dot_general x5 -> x0, matrix products: 8.44 us -> none  [the longest x2 4.38 us: build_ops(): product = jnp.dot(flattened, rotation, preferred_element_type=jnp.float32)]
    add x19 -> x0, other arithmetic: 7.44 us -> none  [the longest x8 6.63 us: pair_velocity(): dist_sq + 2.0 * soft_square]
    dynamic_update_slice x2 -> x0, local copies, waits for them, and re-layouts: 3.12 us -> none  [on_device(): self_ops = lax.map(one_slot, (shapes, quad_weight, live))]
    reshape x8 -> x4, local copies, waits for them, and re-layouts: 0.76 us -> 3.34 us  [the longest x1 1.31 us: on_device(): velocity.reshape(3, slots, n).transpose(1, 0, 2)]
where the time goes in v1:
time: 51 us; the launch traced here: 51.8 us
  Pallas kernels  44.4 us (87%)
  local copies, waits for them, and re-layouts  3.42 us (7%)
  other arithmetic  3.4 us (7%)
  between operations  0.66 us (1%)
    pallas_call x1, Pallas kernels, on_device(): pl.pallas_call(functools.partial(scatter_kernel, slots, grp), out_shape=j...  19.1 us
    pallas_call x1, Pallas kernels, on_device(): pl.pallas_call(functools.partial(gather_kernel, slots, grp, wide, rows),...  17.3 us
    pallas_call x1, Pallas kernels, on_device(): pl.pallas_call(functools.partial(pair_kernel, slots, grp, wide, rows), ou...  7.88 us
    reshape x1, local copies, waits for them, and re-layouts, on_device(): velocity.reshape(3, slots, n).transpose(1, 0, 2)  1.31 us
    reshape x1, local copies, waits for them, and re-layouts, on_device(): flat_density = density.transpose(1, 0, 2).reshape(3 * slots, n)  1.3 us
    concatenate x2, other arithmetic, on_device(): jnp.concatenate([rows_of(shapes), mask, fill, rows_of(strength), jnp.broa...  1.22 us

profile of v1, /device:TPU:0, one launch (start us, length us, event | category | flops | bytes accessed | tf_op | source)
XLA Modules:
  0.0 51.8 jit_solution(5158585584091671853)
XLA Ops:
  0.6 0.7 %convert_element_type.12 = f32[2]{0:T(128)S(1)} convert(s32[2]{0:T(128)} %param.9) | non-fusion elementwise | flops 2 | bytes 16 | tf_op jit(solution)/shard_map/convert_element_type | solution.py:287
  1.3 0.7 %convert_multiply_fusion = f32[2,64]{1,0:T(2,128)S(1)} fusion(s32[2,64]{1,0:T(2,128)} %param.10, f32[2]{0:T(128)S(1)} %convert_element_type.12), kind=kLoop, calls=%fused_computation.9 | loop fusion | flops 256 | bytes 1032 | tf_op jit(solution)/shard_map/mul | solution.py:295
  2.0 0.1 broadcast_in_dim.2
  2.1 0.8 %multiply_bitcast_fusion = f32[3,2,312]{2,1,0:T(2,128)S(1)} fusion(f32[2,3,312]{2,0,1:T(2,128)} %param.7, f32[2]{0:T(128)S(1)} %convert_element_type.12, f32[2,312]{1,0:T(2,128)} %qw_ref.1), kind=kLoop, calls=%fused_computation.8 | loop fusion | flops 3744 | bytes 17480 | tf_op jit(solution)/shard_map/transpose | solution.py:291
  2.9 0.6 %pad_maximum_fusion.live_ref = f32[8,384]{1,0:T(8,128)} fusion(f32[2,384]{1,0:T(2,128)S(1)} %broadcast_in_dim.2, f32[6,384]{1,0:T(8,128)S(1)} %pad.13), kind=kLoop, calls=%fused_computation.7 | loop fusion | flops 3072 | bytes 24576 | tf_op jit(solution)/shard_map/concatenate | solution.py:296
  3.5 0.7 %reshape.19 = f32[6,312]{1,0:T(8,128)S(1)} reshape(f32[3,2,312]{2,1,0:T(2,128)} %bitcast.7) | data formatting | bytes 14976 | tf_op jit(solution)/shard_map/reshape | solution.py:291
  4.2 0.6 %fusion.1.pk_ref = f32[16,384]{1,0:T(8,128)} fusion(f32[2,64]{1,0:T(2,128)S(1)} %convert_multiply_fusion, f32[6,312]{1,0:T(8,128)S(1)} %reshape.19, f32[2,384]{1,0:T(2,128)S(1)} %broadcast_in_dim.2, f32[6,384]{1,0:T(8,128)S(1)} %pad.13), kind=kLoop, calls=%fused_computation.4 | loop fusion | flops 55296 | bytes 44864 | tf_op jit(solution)/shard_map/concatenate | solution.py:296
  4.8 1.3 %reshape.21.dens_ref = f32[6,312]{1,0:T(8,128)} reshape(f32[3,2,312]{2,1,0:T(2,128)} %bitcast.6) | data formatting | bytes 14976 | tf_op jit(solution)/shard_map/reshape | solution.py:303
  6.1 17.3 %gather_ops.1 = (bf16[2,6,312,312]{3,2,1,0:T(8,128)(2,1)}, f32[6,312]{1,0:T(8,128)}, f32[8,8,384]{2,1,0:T(8,128)}, f32[4,16,384]{2,1,0:T(8,128)}, s32[24,128]{1,0:T(8,128)}) custom-call(f32[16,384]{1,0:T(8,128)} %fusion.1.pk_ref, f32[2,312]{1,0:T(2,128)} %qw_ref.1, f32[6,312]{1,0:T(8,128)} %reshape.21.dens_ref, bf16[312,312]{1,0:T(8,128)(2,1)} %rot_ref.1), custom_call_target="tpu_custom_call" | custom-call | tf_op jit(solution)/shard_map/gather_ops/pallas_call | solution.py:306
  23.5 7.9 %pair_sums.1 = (bf16[2,3,3,312,312]{4,3,2,1,0:T(8,128)(2,1)}, f32[8,8,384]{2,1,0:T(8,128)}) custom-call(s32[24,128]{1,0:T(8,128)} %get-tuple-element.9.mask_ref, bf16[2,6,312,312]{3,2,1,0:T(8,128)(2,1)} %get-tuple-element.10.ops_ref, f32[8,8,384]{2,1,0:T(8,128)} %get-tuple-element.11.tgt_ref, f32[4,16,384]{2,1,0:T(8,128)} %get-tuple-element.12.src_ref), custom_call_target="tpu_custom_call" | custom-call | tf_op jit(solution)/shard_map/pair_sums/pallas_call | solution.py:330
  31.4 19.1 %scatter_sums.1 = f32[6,312]{1,0:T(8,128)} custom-call(f32[8,8,384]{2,1,0:T(8,128)} %get-tuple-element.14.part_ref, f32[6,312]{1,0:T(8,128)} %get-tuple-element.15.self_ref, f32[8,384]{1,0:T(8,128)} %pad_maximum_fusion.live_ref), custom_call_target="tpu_custom_call" | custom-call | tf_op jit(solution)/shard_map/scatter_sums/pallas_call | solution.py:348
  50.5 1.3 %reshape.22 = f32[3,2,312]{2,1,0:T(2,128)} reshape(f32[6,312]{1,0:T(8,128)} %scatter_sums.1) | data formatting | bytes 14976 | tf_op jit(solution)/shard_map/reshape | solution.py:363
  (2 shorter events, 0.0 us)
